TPU v7x, 256 devices: a whole 4x4x8 slice. The times are simulated.
256 devices in a mesh: grp: 8 (over x, y_hi), blk: 32 (over z, y_lo, core).
Axes of the slice: x: 4, y: 4 (y_hi: 2, y_lo: 2; y = y_hi * 2 + y_lo), z: 8, core: 2. Of those that a mesh axis runs over, the one named last changes fastest.
Arguments:
- counts: int32 [65536, 1024], P(('grp', 'blk')), may hold values from 0 to 5
- tile_live: int32 [512, 8], P(('grp', 'blk')), may hold values from 0 to 1
- doc_lengths: int32 [65536], P(('grp', 'blk')), may hold values from 256 to 4095
- doc_mix: bfloat16 [65536, 4096], P(('grp', 'blk')), may hold values from 0.019897461 to 50
- word_topic: float32 [4096, 4096], P('blk'), may hold values from 0.01 to 8
- topic_total: float32 [4096], replicated, may hold values from 20000 to 400000
Outputs:
- doc_share: bfloat16 [65536, 4096], P(('grp', 'blk'))
- word_topic_new: float32 [4096, 4096], P('blk')
- topic_mean: float32 [4096], replicated
All inputs are finite; a program needn't handle non-finite values.
Results may differ from a plain program's by a relative error of at most 0.0004.
The roundings to bfloat16 on the way count: a program that leaves them out, or rounds other values in their place, can miss the bound.
Values may be sent and summed in bfloat16 or wider, within the bound.
A program may use at most 128 MiB of HBM per device.

v0:
```python
import jax
import jax.numpy as jnp
from jax import lax
from jax.sharding import PartitionSpec as P

VOCAB = 262144
alpha_prior = 0.1
beta_prior = 0.01


def passed_along(block, axis, distance):
    devices = range(lax.axis_size(axis))
    route = [((i - distance) % len(devices), i) for i in devices]
    return lax.ppermute(block, axis, route)


def tile_terms(operands):
    doc_rows, block_counts, visitor = operands
    normalizer = jnp.dot(doc_rows, visitor.T, preferred_element_type=jnp.float32)
    ratio = (block_counts / normalizer).astype(jnp.bfloat16)
    doc_part = jnp.dot(ratio, visitor, preferred_element_type=jnp.float32)
    word_part = jnp.dot(ratio.T, doc_rows, preferred_element_type=jnp.float32)
    return (doc_part, word_part)


def shard_terms(visitor, block_counts, doc_low):
    return tile_terms((doc_low, block_counts, visitor))


def local(counts, tile_live, doc_lengths, doc_mix, word_topic, topic_total):
    block_rows = word_topic.shape[0]
    visits = tile_live.shape[1]
    word_weight = (word_topic + beta_prior) / (topic_total + beta_prior * VOCAB)[None, :]
    word_low = word_weight.astype(jnp.bfloat16)
    mix_wide = doc_mix.astype(jnp.float32)
    doc_theta = mix_wide / jnp.sum(mix_wide, axis=1, keepdims=True)
    doc_weight = doc_lengths.astype(jnp.float32)[:, None] * doc_theta + alpha_prior
    doc_low = doc_weight.astype(jnp.bfloat16)
    live_full = jnp.repeat(jnp.repeat(tile_live, block_rows, axis=0), block_rows, axis=1)
    live_counts = counts.astype(jnp.float32) * live_full.astype(jnp.float32)
    window_len = jnp.sum(live_counts, axis=1)
    doc_proj = jnp.zeros((doc_low.shape[0], doc_low.shape[1]), jnp.float32)
    word_accum = jnp.zeros((block_rows, doc_low.shape[1]), jnp.float32)
    visitor = word_low
    for offset in range(visits):
        if offset > 0:
            visitor, word_accum = (
                passed_along(visitor.astype(jnp.float32), "blk", -1).astype(visitor.dtype),
                passed_along(word_accum, "blk", -1),
            )
        block_counts = live_counts[:, offset * block_rows : (offset + 1) * block_rows]
        doc_part, word_part = shard_terms(visitor, block_counts, doc_low)
        doc_proj = doc_proj + doc_part
        word_accum = word_accum + word_part
    word_accum = passed_along(word_accum, "blk", visits - 1)
    doc_new = doc_weight * doc_proj
    column_sum = jnp.sum(doc_new, axis=0)
    topic_count = doc_low.shape[1]
    doc_share = (
        topic_count * (doc_new + alpha_prior) / (window_len[:, None] + topic_count * alpha_prior)
    ).astype(jnp.bfloat16)
    word_sum = lax.psum(word_accum, "grp")
    topic_sum = lax.psum(column_sum, ("grp", "blk"))
    vocab_window = block_rows * lax.axis_size("blk")
    return (doc_share, word_weight * word_sum, topic_sum / vocab_window)


def solution(mesh):
    return jax.shard_map(
        local,
        mesh=mesh,
        in_specs=(
            P(("grp", "blk"), None),
            P(("grp", "blk"), None),
            P(("grp", "blk")),
            P(("grp", "blk"), None),
            P("blk", None),
            P(),
        ),
        out_specs=(P(("grp", "blk"), None), P("blk", None), P()),
        check_vma=False,
    )
```

profile of v0, /device:TPU:161, one launch (start us, length us, event | category | flops | bytes accessed | tf_op | source)
XLA Modules:
  0.0 519.2 jit_solution(7656554678656352072)
XLA Ops:
  7.2 0.8 convert_element_type.95
  8.1 2.0 convert_reduce_fusion
  10.0 0.7 broadcast_add_fusion
  10.7 1.0 fusion.8
  11.8 0.3 broadcast_in_dim.5
  12.1 0.3 fusion.38
  12.4 1.0 copy-done
  13.4 0.2 fusion.18
  13.7 0.7 fusion.9
  14.4 0.5 fusion.41
  14.8 0.8 collective-permute-start.7
  15.6 1.5 collective-permute-start
  17.1 34.7 %collective-permute-done = bf16[128,4096]{1,0:T(8,128)(2,1)S(1)} collective-permute-done((bf16[128,4096]{1,0:T(8,128)(2,1)S(1)}, bf16[128,4096]{1,0:T(8,128)(2,1)S(1)}, u32[]{:S(2)}, u32[]{:S(2)}) %collective-permute-start) | collective-permute-done | bytes 1048608 | tf_op jit(solution)/shard_map/ppermute | solution.py:14
  51.7 0.7 fusion.10
  52.5 0.5 convolution_add_fusion.2
  53.0 0.2 collective-permute-start.8
  53.2 2.8 collective-permute-start.1
  56.0 33.8 %collective-permute-done.1 = bf16[128,4096]{1,0:T(8,128)(2,1)S(1)} collective-permute-done((bf16[128,4096]{1,0:T(8,128)(2,1)S(1)}, bf16[128,4096]{1,0:T(8,128)(2,1)S(1)}, u32[]{:S(2)}, u32[]{:S(2)}) %collective-permute-start.1) | collective-permute-done | bytes 1048608 | tf_op jit(solution)/shard_map/ppermute | solution.py:14
  89.8 0.7 fusion.11
  90.5 0.5 fusion.42
  91.0 0.3 add.91
  91.3 1.1 collective-permute-start.9
  92.4 2.8 collective-permute-start.2
  95.2 32.9 %collective-permute-done.2 = bf16[128,4096]{1,0:T(8,128)(2,1)S(1)} collective-permute-done((bf16[128,4096]{1,0:T(8,128)(2,1)S(1)}, bf16[128,4096]{1,0:T(8,128)(2,1)S(1)}, u32[]{:S(2)}, u32[]{:S(2)}) %collective-permute-start.2) | collective-permute-done | bytes 1048608 | tf_op jit(solution)/shard_map/ppermute | solution.py:14
  128.0 0.7 fusion.12
  128.8 0.5 fusion.43
  129.2 0.3 add.92
  129.5 2.0 collective-permute-start.10
  131.5 2.8 collective-permute-start.3
  134.3 32.0 %collective-permute-done.3 = bf16[128,4096]{1,0:T(8,128)(2,1)S(1)} collective-permute-done((bf16[128,4096]{1,0:T(8,128)(2,1)S(1)}, bf16[128,4096]{1,0:T(8,128)(2,1)S(1)}, u32[]{:S(2)}, u32[]{:S(2)}) %collective-permute-start.3) | collective-permute-done | bytes 1048608 | tf_op jit(solution)/shard_map/ppermute | solution.py:14
  166.3 0.7 fusion.13
  167.0 0.5 fusion.44
  167.5 0.3 add.93
  167.7 2.9 collective-permute-start.11
  170.6 2.8 collective-permute-start.4
  173.4 31.1 %collective-permute-done.4 = bf16[128,4096]{1,0:T(8,128)(2,1)S(1)} collective-permute-done((bf16[128,4096]{1,0:T(8,128)(2,1)S(1)}, bf16[128,4096]{1,0:T(8,128)(2,1)S(1)}, u32[]{:S(2)}, u32[]{:S(2)}) %collective-permute-start.4) | collective-permute-done | bytes 1048608 | tf_op jit(solution)/shard_map/ppermute | solution.py:14
  204.5 0.7 fusion.14
  205.2 0.5 fusion.45
  205.7 0.3 add.94
  206.0 3.8 collective-permute-start.12
  209.8 2.8 collective-permute-start.5
  212.6 30.2 %collective-permute-done.5 = bf16[128,4096]{1,0:T(8,128)(2,1)S(1)} collective-permute-done((bf16[128,4096]{1,0:T(8,128)(2,1)S(1)}, bf16[128,4096]{1,0:T(8,128)(2,1)S(1)}, u32[]{:S(2)}, u32[]{:S(2)}) %collective-permute-start.5) | collective-permute-done | bytes 1048608 | tf_op jit(solution)/shard_map/ppermute | solution.py:14
  242.7 0.7 fusion.15
  243.5 0.5 fusion.46
  243.9 0.3 add.95
  244.2 4.7 collective-permute-start.13
  248.9 2.8 collective-permute-start.6
  251.7 0.7 fusion.40
  252.4 28.6 %collective-permute-done.6 = bf16[128,4096]{1,0:T(8,128)(2,1)S(1)} collective-permute-done((bf16[128,4096]{1,0:T(8,128)(2,1)S(1)}, bf16[128,4096]{1,0:T(8,128)(2,1)S(1)}, u32[]{:S(2)}, u32[]{:S(2)}) %collective-permute-start.6) | collective-permute-done | bytes 1048608 | tf_op jit(solution)/shard_map/ppermute | solution.py:14
  281.0 0.7 fusion.16
  281.7 0.5 fusion.47
  282.2 0.2 add.96
  282.4 6.9 %collective-permute-start.14 = (f32[128,4096]{1,0:T(8,128)S(1)}, f32[128,4096]{1,0:T(8,128)}, u32[]{:S(2)}, u32[]{:S(2)}) collective-permute-start(f32[128,4096]{1,0:T(8,128)S(1)} %add.96), channel_id=1, source_target_pairs={{25,0},{26,1},{27,2},{28,3},{29,4},{30,5},{31,6},{0,7},{1,8},{2,9}... | collective-permute-start | bytes 6291464 | tf_op jit(solution)/shard_map/ppermute | solution.py:14
  289.3 2.7 convolution_add_fusion.1
  292.0 2.6 fusion.52
  294.6 2.6 fusion.51
  297.2 2.7 fusion.50
  299.9 2.7 fusion.49
  302.6 2.6 fusion.48
  305.2 69.0 %collective-permute-done.14 = f32[128,4096]{1,0:T(8,128)} collective-permute-done((f32[128,4096]{1,0:T(8,128)S(1)}, f32[128,4096]{1,0:T(8,128)}, u32[]{:S(2)}, u32[]{:S(2)}) %collective-permute-start.14) | collective-permute-done | bytes 2097184 | tf_op jit(solution)/shard_map/ppermute | solution.py:14
  374.2 11.5 %fusion.39 = (f32[4096]{0:T(1024)S(1)}, bf16[256,4096]{1,0:T(8,128)(2,1)}) fusion(f32[256]{0:T(256)S(1)} %broadcast_add_fusion.1, f32[256,4096]{1,0:T(8,128)} %fusion.48, f32[256,4096]{1,0:T(8,128)} %fusion.49, f32[256,4096]{1,0:T(8,128)} %fusion.50, f32[256,4096]{1,0:T(8,128)} %fusion.51, f32[256,4096]{1,0:T(8,128)} %fusion.52, ...), kind=kOutput, calls=%fused_computation.64 | convolution fusion | flops 285208576 | bytes 30493696 | tf_op jit(solution)/shard_map/dot_general | solution.py:21
  385.7 122.8 %psum.15 = f32[4096]{0:T(1024)S(1)} all-reduce(f32[4096]{0:T(1024)S(1)} %get-tuple-element.5), channel_id=1, replica_groups=mesh['grp'=8,'blk'=32] {'grp','blk'}, use_global_device_ids=true, to_apply=%region_4.0 | all-reduce | flops 4096 | bytes 32768 | tf_op jit(solution)/shard_map/psum | solution.py:63
  508.5 0.6 broadcast_multiply_fusion
  509.1 3.2 fusion.17
  (20 shorter events, 0.1 us)
Async XLA Ops:
  7.2 3.6 copy-start.1
  7.2 2.8 copy-start.3
  7.2 501.9 %all-reduce.2.cloned.1.call-start = ((), (), s32[]{:S(2)}) async-start(), calls=%async_computation | async-start | bytes 4194304 | tf_op jit(solution)/shard_map/psum | solution.py:62
  10.7 1.4 copy-start.2
  11.8 1.6 copy-start
  14.8 37.6 %collective-permute-start.7 = (f32[128,4096]{1,0:T(8,128)S(1)}, f32[128,4096]{1,0:T(8,128)S(1)}, u32[]{:S(2)}, u32[]{:S(2)}) collective-permute-start(f32[128,4096]{1,0:T(8,128)S(1)} %fusion.41), channel_id=1, source_target_pairs={{1,0},{2,1},{3,2},{4,3},{5,4},{6,5},{7,6},{8,7},{9,8},{10,9},{11,1... | collective-permute-start | bytes 6291464 | tf_op jit(solution)/shard_map/ppermute | solution.py:14
  15.6 36.1 %collective-permute-start = (bf16[128,4096]{1,0:T(8,128)(2,1)S(1)}, bf16[128,4096]{1,0:T(8,128)(2,1)S(1)}, u32[]{:S(2)}, u32[]{:S(2)}) collective-permute-start(bf16[128,4096]{1,0:T(8,128)(2,1)S(1)} %fusion.18), channel_id=1, source_target_pairs={{1,0},{2,1},{3,2},{4,3},{5,4},{6,5},{7,6},{8,7},{9,8},{10,9},{11,1... | collective-permute-start | bytes 3145736 | tf_op jit(solution)/shard_map/ppermute | solution.py:14
  53.0 38.0 %collective-permute-start.8 = (f32[128,4096]{1,0:T(8,128)S(1)}, f32[128,4096]{1,0:T(8,128)S(1)}, u32[]{:S(2)}, u32[]{:S(2)}) collective-permute-start(f32[128,4096]{1,0:T(8,128)S(1)} %convolution_add_fusion.2), channel_id=1, source_target_pairs={{1,0},{2,1},{3,2},{4,3},{5,4},{6,5},{7,6},{8,7},{9,8},{10,9},{11,1... | collective-permute-start | bytes 6291464 | tf_op jit(solution)/shard_map/ppermute | solution.py:14
  53.2 36.6 %collective-permute-start.1 = (bf16[128,4096]{1,0:T(8,128)(2,1)S(1)}, bf16[128,4096]{1,0:T(8,128)(2,1)S(1)}, u32[]{:S(2)}, u32[]{:S(2)}) collective-permute-start(bf16[128,4096]{1,0:T(8,128)(2,1)S(1)} %collective-permute-done), channel_id=1, source_target_pairs={{1,0},{2,1},{3,2},{4,3},{5,4},{6,5},{7,6},{8,7},{9,8},{10,9},{11,1... | collective-permute-start | bytes 3145736 | tf_op jit(solution)/shard_map/ppermute | solution.py:14
  91.3 38.0 %collective-permute-start.9 = (f32[128,4096]{1,0:T(8,128)S(1)}, f32[128,4096]{1,0:T(8,128)S(1)}, u32[]{:S(2)}, u32[]{:S(2)}) collective-permute-start(f32[128,4096]{1,0:T(8,128)S(1)} %add.91), channel_id=1, source_target_pairs={{1,0},{2,1},{3,2},{4,3},{5,4},{6,5},{7,6},{8,7},{9,8},{10,9},{11,1... | collective-permute-start | bytes 6291464 | tf_op jit(solution)/shard_map/ppermute | solution.py:14
  92.4 35.7 %collective-permute-start.2 = (bf16[128,4096]{1,0:T(8,128)(2,1)S(1)}, bf16[128,4096]{1,0:T(8,128)(2,1)S(1)}, u32[]{:S(2)}, u32[]{:S(2)}) collective-permute-start(bf16[128,4096]{1,0:T(8,128)(2,1)S(1)} %collective-permute-done.1), channel_id=1, source_target_pairs={{1,0},{2,1},{3,2},{4,3},{5,4},{6,5},{7,6},{8,7},{9,8},{10,9},{11,1... | collective-permute-start | bytes 3145736 | tf_op jit(solution)/shard_map/ppermute | solution.py:14
  129.5 38.0 %collective-permute-start.10 = (f32[128,4096]{1,0:T(8,128)S(1)}, f32[128,4096]{1,0:T(8,128)S(1)}, u32[]{:S(2)}, u32[]{:S(2)}) collective-permute-start(f32[128,4096]{1,0:T(8,128)S(1)} %add.92), channel_id=1, source_target_pairs={{1,0},{2,1},{3,2},{4,3},{5,4},{6,5},{7,6},{8,7},{9,8},{10,9},{11,1... | collective-permute-start | bytes 6291464 | tf_op jit(solution)/shard_map/ppermute | solution.py:14
  131.5 34.8 %collective-permute-start.3 = (bf16[128,4096]{1,0:T(8,128)(2,1)S(1)}, bf16[128,4096]{1,0:T(8,128)(2,1)S(1)}, u32[]{:S(2)}, u32[]{:S(2)}) collective-permute-start(bf16[128,4096]{1,0:T(8,128)(2,1)S(1)} %collective-permute-done.2), channel_id=1, source_target_pairs={{1,0},{2,1},{3,2},{4,3},{5,4},{6,5},{7,6},{8,7},{9,8},{10,9},{11,1... | collective-permute-start | bytes 3145736 | tf_op jit(solution)/shard_map/ppermute | solution.py:14
  167.7 38.0 %collective-permute-start.11 = (f32[128,4096]{1,0:T(8,128)S(1)}, f32[128,4096]{1,0:T(8,128)S(1)}, u32[]{:S(2)}, u32[]{:S(2)}) collective-permute-start(f32[128,4096]{1,0:T(8,128)S(1)} %add.93), channel_id=1, source_target_pairs={{1,0},{2,1},{3,2},{4,3},{5,4},{6,5},{7,6},{8,7},{9,8},{10,9},{11,1... | collective-permute-start | bytes 6291464 | tf_op jit(solution)/shard_map/ppermute | solution.py:14
  170.6 33.9 %collective-permute-start.4 = (bf16[128,4096]{1,0:T(8,128)(2,1)S(1)}, bf16[128,4096]{1,0:T(8,128)(2,1)S(1)}, u32[]{:S(2)}, u32[]{:S(2)}) collective-permute-start(bf16[128,4096]{1,0:T(8,128)(2,1)S(1)} %collective-permute-done.3), channel_id=1, source_target_pairs={{1,0},{2,1},{3,2},{4,3},{5,4},{6,5},{7,6},{8,7},{9,8},{10,9},{11,1... | collective-permute-start | bytes 3145736 | tf_op jit(solution)/shard_map/ppermute | solution.py:14
  206.0 38.0 %collective-permute-start.12 = (f32[128,4096]{1,0:T(8,128)S(1)}, f32[128,4096]{1,0:T(8,128)S(1)}, u32[]{:S(2)}, u32[]{:S(2)}) collective-permute-start(f32[128,4096]{1,0:T(8,128)S(1)} %add.94), channel_id=1, source_target_pairs={{1,0},{2,1},{3,2},{4,3},{5,4},{6,5},{7,6},{8,7},{9,8},{10,9},{11,1... | collective-permute-start | bytes 6291464 | tf_op jit(solution)/shard_map/ppermute | solution.py:14
  209.8 33.0 %collective-permute-start.5 = (bf16[128,4096]{1,0:T(8,128)(2,1)S(1)}, bf16[128,4096]{1,0:T(8,128)(2,1)S(1)}, u32[]{:S(2)}, u32[]{:S(2)}) collective-permute-start(bf16[128,4096]{1,0:T(8,128)(2,1)S(1)} %collective-permute-done.4), channel_id=1, source_target_pairs={{1,0},{2,1},{3,2},{4,3},{5,4},{6,5},{7,6},{8,7},{9,8},{10,9},{11,1... | collective-permute-start | bytes 3145736 | tf_op jit(solution)/shard_map/ppermute | solution.py:14
  244.2 38.0 %collective-permute-start.13 = (f32[128,4096]{1,0:T(8,128)S(1)}, f32[128,4096]{1,0:T(8,128)S(1)}, u32[]{:S(2)}, u32[]{:S(2)}) collective-permute-start(f32[128,4096]{1,0:T(8,128)S(1)} %add.95), channel_id=1, source_target_pairs={{1,0},{2,1},{3,2},{4,3},{5,4},{6,5},{7,6},{8,7},{9,8},{10,9},{11,1... | collective-permute-start | bytes 6291464 | tf_op jit(solution)/shard_map/ppermute | solution.py:14
  248.9 32.1 %collective-permute-start.6 = (bf16[128,4096]{1,0:T(8,128)(2,1)S(1)}, bf16[128,4096]{1,0:T(8,128)(2,1)S(1)}, u32[]{:S(2)}, u32[]{:S(2)}) collective-permute-start(bf16[128,4096]{1,0:T(8,128)(2,1)S(1)} %collective-permute-done.5), channel_id=1, source_target_pairs={{1,0},{2,1},{3,2},{4,3},{5,4},{6,5},{7,6},{8,7},{9,8},{10,9},{11,1... | collective-permute-start | bytes 3145736 | tf_op jit(solution)/shard_map/ppermute | solution.py:14
  282.4 91.8 %collective-permute-start.14 = (f32[128,4096]{1,0:T(8,128)S(1)}, f32[128,4096]{1,0:T(8,128)}, u32[]{:S(2)}, u32[]{:S(2)}) collective-permute-start(f32[128,4096]{1,0:T(8,128)S(1)} %add.96), channel_id=1, source_target_pairs={{25,0},{26,1},{27,2},{28,3},{29,4},{30,5},{31,6},{0,7},{1,8},{2,9}... | collective-permute-start | bytes 6291464 | tf_op jit(solution)/shard_map/ppermute | solution.py:14
Sparse Core Ops, SparseCore 0:
  374.3 117.2 all-reduce.1
where the time goes:
time: 520 us; the launch traced here: 519 us
  waiting for transfers between devices  292 us (56%)
  blocking collectives  123 us (24%)
  starting transfers between devices  40.6 us (8%)
  matrix products  37.6 us (7%)
  between operations  14.3 us (3%)
  other arithmetic  10.4 us (2%)
    ppermute x15, waiting for transfers between devices, passed_along(): return lax.ppermute(block, axis, route)  292 us
    psum x1, blocking collectives, local(): topic_sum = lax.psum(column_sum, ('grp', 'blk'))  123 us
    ppermute x15, starting transfers between devices, passed_along(): return lax.ppermute(block, axis, route)  40.6 us
    dot_general x8, matrix products, tile_terms(): doc_part = jnp.dot(ratio, visitor, preferred_element_type=jnp.float32)  28.1 us
  transfers between devices with their start and end apart: 16, of which 8 were waited for; matrix products, arithmetic and copies ran while one was open for 7% of the time, Pallas kernels for 0%

commit v1 on v0

--- a/solution.py
+++ b/solution.py
@@ -60,7 +60,7 @@
         topic_count * (doc_new + alpha_prior) / (window_len[:, None] + topic_count * alpha_prior)
     ).astype(jnp.bfloat16)
     word_sum = lax.psum(word_accum, "grp")
-    topic_sum = lax.psum(column_sum, ("grp", "blk"))
+    topic_sum = lax.psum(lax.psum(column_sum, "grp"), "blk")
     vocab_window = block_rows * lax.axis_size("blk")
     return (doc_share, word_weight * word_sum, topic_sum / vocab_window)
 

time: 520 us -> 548 us (1.054)
  the two profiles are of different devices: /device:TPU:161 before, /device:TPU:0 now
where the time goes in v1:
time: 548 us
  waiting for transfers between devices  294 us (54%)
  blocking collectives  159 us (29%)
  matrix products  37.6 us (7%)
  starting transfers between devices  31 us (6%)
  between operations  14.3 us (3%)
  other arithmetic  10.4 us (2%)
    ppermute x15, waiting for transfers between devices, passed_along(): return lax.ppermute(block, axis, route)  294 us
    psum x2, blocking collectives, local(): topic_sum = lax.psum(lax.psum(column_sum, 'grp'), 'blk')  159 us
    ppermute x15, starting transfers between devices, passed_along(): return lax.ppermute(block, axis, route)  31 us
    dot_general x8, matrix products, tile_terms(): doc_part = jnp.dot(ratio, visitor, preferred_element_type=jnp.float32)  28.1 us
  transfers between devices with their start and end apart: 16, of which 8 were waited for; matrix products, arithmetic and copies ran while one was open for 7% of the time, Pallas kernels for 0%

profile of v1, /device:TPU:0, one launch (start us, length us, event | category | flops | bytes accessed | tf_op | source)
XLA Modules:
  0.0 547.8 jit_solution(11739202382619594094)
XLA Ops:
  7.2 0.8 convert_element_type.95
  8.1 2.0 convert_reduce_fusion
  10.0 0.7 broadcast_add_fusion
  10.7 1.0 fusion.8
  11.8 0.3 broadcast_in_dim.5
  12.1 0.3 fusion.38
  12.4 1.0 copy-done
  13.4 0.2 fusion.18
  13.7 0.7 fusion.9
  14.4 0.5 fusion.41
  14.9 4.7 collective-permute-start.7
  19.5 0.7 collective-permute-start
  20.2 34.1 %collective-permute-done = bf16[128,4096]{1,0:T(8,128)(2,1)S(1)} collective-permute-done((bf16[128,4096]{1,0:T(8,128)(2,1)S(1)}, bf16[128,4096]{1,0:T(8,128)(2,1)S(1)}, u32[]{:S(2)}, u32[]{:S(2)}) %collective-permute-start) | collective-permute-done | bytes 1048608 | tf_op jit(solution)/shard_map/ppermute | solution.py:14
  54.3 0.7 fusion.10
  55.0 0.5 convolution_add_fusion.2
  55.6 4.1 collective-permute-start.8
  59.7 0.1 collective-permute-start.1
  59.8 34.7 %collective-permute-done.1 = bf16[128,4096]{1,0:T(8,128)(2,1)S(1)} collective-permute-done((bf16[128,4096]{1,0:T(8,128)(2,1)S(1)}, bf16[128,4096]{1,0:T(8,128)(2,1)S(1)}, u32[]{:S(2)}, u32[]{:S(2)}) %collective-permute-start.1) | collective-permute-done | bytes 1048608 | tf_op jit(solution)/shard_map/ppermute | solution.py:14
  94.5 0.7 fusion.11
  95.2 0.5 fusion.42
  95.7 0.3 add.93
  95.9 4.1 collective-permute-start.9
  100.0 0.1 collective-permute-start.2
  100.1 34.7 %collective-permute-done.2 = bf16[128,4096]{1,0:T(8,128)(2,1)S(1)} collective-permute-done((bf16[128,4096]{1,0:T(8,128)(2,1)S(1)}, bf16[128,4096]{1,0:T(8,128)(2,1)S(1)}, u32[]{:S(2)}, u32[]{:S(2)}) %collective-permute-start.2) | collective-permute-done | bytes 1048608 | tf_op jit(solution)/shard_map/ppermute | solution.py:14
  134.8 0.7 fusion.12
  135.5 0.5 fusion.43
  136.0 0.3 add.94
  136.3 4.1 collective-permute-start.10
  140.4 0.3 collective-permute-start.3
  140.7 34.5 %collective-permute-done.3 = bf16[128,4096]{1,0:T(8,128)(2,1)S(1)} collective-permute-done((bf16[128,4096]{1,0:T(8,128)(2,1)S(1)}, bf16[128,4096]{1,0:T(8,128)(2,1)S(1)}, u32[]{:S(2)}, u32[]{:S(2)}) %collective-permute-start.3) | collective-permute-done | bytes 1048608 | tf_op jit(solution)/shard_map/ppermute | solution.py:14
  175.2 0.7 fusion.13
  175.9 0.5 fusion.44
  176.4 0.3 add.95
  176.6 4.1 collective-permute-start.11
  180.7 0.1 collective-permute-start.4
  180.8 34.7 %collective-permute-done.4 = bf16[128,4096]{1,0:T(8,128)(2,1)S(1)} collective-permute-done((bf16[128,4096]{1,0:T(8,128)(2,1)S(1)}, bf16[128,4096]{1,0:T(8,128)(2,1)S(1)}, u32[]{:S(2)}, u32[]{:S(2)}) %collective-permute-start.4) | collective-permute-done | bytes 1048608 | tf_op jit(solution)/shard_map/ppermute | solution.py:14
  215.5 0.7 fusion.14
  216.2 0.5 fusion.45
  216.7 0.3 add.96
  217.0 4.1 collective-permute-start.12
  221.1 0.1 collective-permute-start.5
  221.2 34.7 %collective-permute-done.5 = bf16[128,4096]{1,0:T(8,128)(2,1)S(1)} collective-permute-done((bf16[128,4096]{1,0:T(8,128)(2,1)S(1)}, bf16[128,4096]{1,0:T(8,128)(2,1)S(1)}, u32[]{:S(2)}, u32[]{:S(2)}) %collective-permute-start.5) | collective-permute-done | bytes 1048608 | tf_op jit(solution)/shard_map/ppermute | solution.py:14
  255.9 0.7 fusion.15
  256.6 0.5 fusion.46
  257.1 0.3 add.97
  257.3 4.1 collective-permute-start.13
  261.5 0.7 fusion.40
  262.2 34.0 %collective-permute-done.6 = bf16[128,4096]{1,0:T(8,128)(2,1)S(1)} collective-permute-done((bf16[128,4096]{1,0:T(8,128)(2,1)S(1)}, bf16[128,4096]{1,0:T(8,128)(2,1)S(1)}, u32[]{:S(2)}, u32[]{:S(2)}) %collective-permute-start.6) | collective-permute-done | bytes 1048608 | tf_op jit(solution)/shard_map/ppermute | solution.py:14
  296.2 0.7 fusion.16
  296.9 0.5 fusion.47
  297.4 0.2 add.98
  297.7 0.3 collective-permute-start.14
  298.0 2.7 convolution_add_fusion.1
  300.6 2.6 fusion.52
  303.3 2.6 fusion.51
  305.9 2.7 fusion.50
  308.6 2.7 fusion.49
  311.2 2.6 fusion.48
  313.9 52.7 %collective-permute-done.14 = f32[128,4096]{1,0:T(8,128)} collective-permute-done((f32[128,4096]{1,0:T(8,128)S(1)}, f32[128,4096]{1,0:T(8,128)}, u32[]{:S(2)}, u32[]{:S(2)}) %collective-permute-start.14) | collective-permute-done | bytes 2097184 | tf_op jit(solution)/shard_map/ppermute | solution.py:14
  366.6 11.5 %fusion.39 = (f32[4096]{0:T(1024)S(1)}, bf16[256,4096]{1,0:T(8,128)(2,1)}) fusion(f32[256]{0:T(256)S(1)} %broadcast_add_fusion.1, f32[256,4096]{1,0:T(8,128)} %fusion.48, f32[256,4096]{1,0:T(8,128)} %fusion.49, f32[256,4096]{1,0:T(8,128)} %fusion.50, f32[256,4096]{1,0:T(8,128)} %fusion.51, f32[256,4096]{1,0:T(8,128)} %fusion.52, ...), kind=kOutput, calls=%fused_computation.64 | convolution fusion | flops 285208576 | bytes 30493696 | tf_op jit(solution)/shard_map/dot_general | solution.py:21
  378.1 41.7 %psum.22 = f32[4096]{0:T(1024)S(1)} all-reduce(f32[4096]{0:T(1024)S(1)} %get-tuple-element.5), channel_id=1, replica_groups=mesh['grp'=8,'blk'=32] {'grp'}, use_global_device_ids=true, to_apply=%region_4.0 | all-reduce | flops 4096 | bytes 32768 | tf_op jit(solution)/shard_map/psum | solution.py:63
  419.8 117.4 %psum.23 = f32[4096]{0:T(1024)S(1)} all-reduce(f32[4096]{0:T(1024)S(1)} %psum.22), channel_id=1, replica_groups=mesh['grp'=8,'blk'=32] {'blk'}, use_global_device_ids=true, to_apply=%region_5.0 | all-reduce | flops 4096 | bytes 32768 | tf_op jit(solution)/shard_map/psum | solution.py:63
  537.2 0.6 broadcast_multiply_fusion
  537.8 3.2 fusion.17
  (21 shorter events, 0.2 us)
Async XLA Ops:
  7.2 3.6 copy-start.1
  7.2 2.8 copy-start.3
  7.2 530.6 %all-reduce.2.cloned.1.call-start = ((), (), s32[]{:S(2)}) async-start(), calls=%async_computation | async-start | bytes 4194304 | tf_op jit(solution)/shard_map/psum | solution.py:62
  10.7 1.4 copy-start.2
  11.8 1.6 copy-start
  14.9 40.2 %collective-permute-start.7 = (f32[128,4096]{1,0:T(8,128)S(1)}, f32[128,4096]{1,0:T(8,128)S(1)}, u32[]{:S(2)}, u32[]{:S(2)}) collective-permute-start(f32[128,4096]{1,0:T(8,128)S(1)} %fusion.41), channel_id=1, source_target_pairs={{1,0},{2,1},{3,2},{4,3},{5,4},{6,5},{7,6},{8,7},{9,8},{10,9},{11,1... | collective-permute-start | bytes 6291464 | tf_op jit(solution)/shard_map/ppermute | solution.py:14
  19.5 34.8 %collective-permute-start = (bf16[128,4096]{1,0:T(8,128)(2,1)S(1)}, bf16[128,4096]{1,0:T(8,128)(2,1)S(1)}, u32[]{:S(2)}, u32[]{:S(2)}) collective-permute-start(bf16[128,4096]{1,0:T(8,128)(2,1)S(1)} %fusion.18), channel_id=1, source_target_pairs={{1,0},{2,1},{3,2},{4,3},{5,4},{6,5},{7,6},{8,7},{9,8},{10,9},{11,1... | collective-permute-start | bytes 3145736 | tf_op jit(solution)/shard_map/ppermute | solution.py:14
  55.6 40.1 %collective-permute-start.8 = (f32[128,4096]{1,0:T(8,128)S(1)}, f32[128,4096]{1,0:T(8,128)S(1)}, u32[]{:S(2)}, u32[]{:S(2)}) collective-permute-start(f32[128,4096]{1,0:T(8,128)S(1)} %convolution_add_fusion.2), channel_id=1, source_target_pairs={{1,0},{2,1},{3,2},{4,3},{5,4},{6,5},{7,6},{8,7},{9,8},{10,9},{11,1... | collective-permute-start | bytes 6291464 | tf_op jit(solution)/shard_map/ppermute | solution.py:14
  59.7 34.8 %collective-permute-start.1 = (bf16[128,4096]{1,0:T(8,128)(2,1)S(1)}, bf16[128,4096]{1,0:T(8,128)(2,1)S(1)}, u32[]{:S(2)}, u32[]{:S(2)}) collective-permute-start(bf16[128,4096]{1,0:T(8,128)(2,1)S(1)} %collective-permute-done), channel_id=1, source_target_pairs={{1,0},{2,1},{3,2},{4,3},{5,4},{6,5},{7,6},{8,7},{9,8},{10,9},{11,1... | collective-permute-start | bytes 3145736 | tf_op jit(solution)/shard_map/ppermute | solution.py:14
  95.9 40.1 %collective-permute-start.9 = (f32[128,4096]{1,0:T(8,128)S(1)}, f32[128,4096]{1,0:T(8,128)S(1)}, u32[]{:S(2)}, u32[]{:S(2)}) collective-permute-start(f32[128,4096]{1,0:T(8,128)S(1)} %add.93), channel_id=1, source_target_pairs={{1,0},{2,1},{3,2},{4,3},{5,4},{6,5},{7,6},{8,7},{9,8},{10,9},{11,1... | collective-permute-start | bytes 6291464 | tf_op jit(solution)/shard_map/ppermute | solution.py:14
  100.0 34.8 %collective-permute-start.2 = (bf16[128,4096]{1,0:T(8,128)(2,1)S(1)}, bf16[128,4096]{1,0:T(8,128)(2,1)S(1)}, u32[]{:S(2)}, u32[]{:S(2)}) collective-permute-start(bf16[128,4096]{1,0:T(8,128)(2,1)S(1)} %collective-permute-done.1), channel_id=1, source_target_pairs={{1,0},{2,1},{3,2},{4,3},{5,4},{6,5},{7,6},{8,7},{9,8},{10,9},{11,1... | collective-permute-start | bytes 3145736 | tf_op jit(solution)/shard_map/ppermute | solution.py:14
  136.3 40.1 %collective-permute-start.10 = (f32[128,4096]{1,0:T(8,128)S(1)}, f32[128,4096]{1,0:T(8,128)S(1)}, u32[]{:S(2)}, u32[]{:S(2)}) collective-permute-start(f32[128,4096]{1,0:T(8,128)S(1)} %add.94), channel_id=1, source_target_pairs={{1,0},{2,1},{3,2},{4,3},{5,4},{6,5},{7,6},{8,7},{9,8},{10,9},{11,1... | collective-permute-start | bytes 6291464 | tf_op jit(solution)/shard_map/ppermute | solution.py:14
  140.4 34.8 %collective-permute-start.3 = (bf16[128,4096]{1,0:T(8,128)(2,1)S(1)}, bf16[128,4096]{1,0:T(8,128)(2,1)S(1)}, u32[]{:S(2)}, u32[]{:S(2)}) collective-permute-start(bf16[128,4096]{1,0:T(8,128)(2,1)S(1)} %collective-permute-done.2), channel_id=1, source_target_pairs={{1,0},{2,1},{3,2},{4,3},{5,4},{6,5},{7,6},{8,7},{9,8},{10,9},{11,1... | collective-permute-start | bytes 3145736 | tf_op jit(solution)/shard_map/ppermute | solution.py:14
  176.6 40.1 %collective-permute-start.11 = (f32[128,4096]{1,0:T(8,128)S(1)}, f32[128,4096]{1,0:T(8,128)S(1)}, u32[]{:S(2)}, u32[]{:S(2)}) collective-permute-start(f32[128,4096]{1,0:T(8,128)S(1)} %add.95), channel_id=1, source_target_pairs={{1,0},{2,1},{3,2},{4,3},{5,4},{6,5},{7,6},{8,7},{9,8},{10,9},{11,1... | collective-permute-start | bytes 6291464 | tf_op jit(solution)/shard_map/ppermute | solution.py:14
  180.7 34.8 %collective-permute-start.4 = (bf16[128,4096]{1,0:T(8,128)(2,1)S(1)}, bf16[128,4096]{1,0:T(8,128)(2,1)S(1)}, u32[]{:S(2)}, u32[]{:S(2)}) collective-permute-start(bf16[128,4096]{1,0:T(8,128)(2,1)S(1)} %collective-permute-done.3), channel_id=1, source_target_pairs={{1,0},{2,1},{3,2},{4,3},{5,4},{6,5},{7,6},{8,7},{9,8},{10,9},{11,1... | collective-permute-start | bytes 3145736 | tf_op jit(solution)/shard_map/ppermute | solution.py:14
  217.0 40.1 %collective-permute-start.12 = (f32[128,4096]{1,0:T(8,128)S(1)}, f32[128,4096]{1,0:T(8,128)S(1)}, u32[]{:S(2)}, u32[]{:S(2)}) collective-permute-start(f32[128,4096]{1,0:T(8,128)S(1)} %add.96), channel_id=1, source_target_pairs={{1,0},{2,1},{3,2},{4,3},{5,4},{6,5},{7,6},{8,7},{9,8},{10,9},{11,1... | collective-permute-start | bytes 6291464 | tf_op jit(solution)/shard_map/ppermute | solution.py:14
  221.1 34.8 %collective-permute-start.5 = (bf16[128,4096]{1,0:T(8,128)(2,1)S(1)}, bf16[128,4096]{1,0:T(8,128)(2,1)S(1)}, u32[]{:S(2)}, u32[]{:S(2)}) collective-permute-start(bf16[128,4096]{1,0:T(8,128)(2,1)S(1)} %collective-permute-done.4), channel_id=1, source_target_pairs={{1,0},{2,1},{3,2},{4,3},{5,4},{6,5},{7,6},{8,7},{9,8},{10,9},{11,1... | collective-permute-start | bytes 3145736 | tf_op jit(solution)/shard_map/ppermute | solution.py:14
  257.3 40.1 %collective-permute-start.13 = (f32[128,4096]{1,0:T(8,128)S(1)}, f32[128,4096]{1,0:T(8,128)S(1)}, u32[]{:S(2)}, u32[]{:S(2)}) collective-permute-start(f32[128,4096]{1,0:T(8,128)S(1)} %add.97), channel_id=1, source_target_pairs={{1,0},{2,1},{3,2},{4,3},{5,4},{6,5},{7,6},{8,7},{9,8},{10,9},{11,1... | collective-permute-start | bytes 6291464 | tf_op jit(solution)/shard_map/ppermute | solution.py:14
  261.4 34.8 %collective-permute-start.6 = (bf16[128,4096]{1,0:T(8,128)(2,1)S(1)}, bf16[128,4096]{1,0:T(8,128)(2,1)S(1)}, u32[]{:S(2)}, u32[]{:S(2)}) collective-permute-start(bf16[128,4096]{1,0:T(8,128)(2,1)S(1)} %collective-permute-done.5), channel_id=1, source_target_pairs={{1,0},{2,1},{3,2},{4,3},{5,4},{6,5},{7,6},{8,7},{9,8},{10,9},{11,1... | collective-permute-start | bytes 3145736 | tf_op jit(solution)/shard_map/ppermute | solution.py:14
  297.7 68.9 %collective-permute-start.14 = (f32[128,4096]{1,0:T(8,128)S(1)}, f32[128,4096]{1,0:T(8,128)}, u32[]{:S(2)}, u32[]{:S(2)}) collective-permute-start(f32[128,4096]{1,0:T(8,128)S(1)} %add.98), channel_id=1, source_target_pairs={{25,0},{26,1},{27,2},{28,3},{29,4},{30,5},{31,6},{0,7},{1,8},{2,9}... | collective-permute-start | bytes 6291464 | tf_op jit(solution)/shard_map/ppermute | solution.py:14
Sparse Core Ops, SparseCore 0:
  366.7 128.9 all-reduce.1
